TPU v7x, 32 devices: a whole 2x2x4 slice. The times are simulated.
32 devices in a mesh: groups: 2 (over x), row: 16 (over z, y, core).
Axes of the slice: x: 2, y: 2, z: 4, core: 2. Of those that a mesh axis runs over, the one named last changes fastest.
Arguments:
- orbitals: bfloat16 [4096, 512], P(('groups', 'row')), parts along dimension 0, may hold values from -1.296875 to 1.296875
- basis: bfloat16 [4096, 1024], P(('groups', 'row')), parts along dimension 0, may hold values from -0.1875 to 0.1875
- kernel: bfloat16 [4096, 2048], P(('groups', 'row')), parts along dimension 0, may hold values from -6 to 6
Outputs:
- exchange_matrix: float32 [2048, 1024], P('groups', 'row'), parts along dimension 0
There are 2 independent parts, one for each index of `groups`. A program takes and returns all parts, laid end to end along the dimension named above; each array names one. Nothing has to cross between parts.
All inputs are finite; a program needn't handle non-finite values.
Results may differ from a plain program's by a relative error of at most 0.0041.
Values may be sent and summed in bfloat16 or wider, within the bound.
A program may use at most 128 MiB of HBM per device.

v0:
```python
import jax
import jax.numpy as jnp
from jax import lax
from jax.sharding import PartitionSpec as P


def shards(orbitals, basis, kernel):
    density = lax.dot_general(
        orbitals,
        lax.all_gather(orbitals, "row", axis=0, tiled=True),
        (((1,), (1,)), ((), ())),
        preferred_element_type=jnp.float32,
    )
    weighted = (density * kernel.astype(jnp.float32)).astype(jnp.bfloat16)
    whole_basis = lax.all_gather(basis, "row", axis=0, tiled=True)
    applied = jnp.dot(weighted, whole_basis, preferred_element_type=jnp.float32).astype(
        jnp.bfloat16
    )
    received = lax.all_to_all(applied, "row", split_axis=1, concat_axis=0, tiled=True)
    exchange_matrix = lax.dot_general(
        whole_basis, received, (((0,), (0,)), ((), ())), preferred_element_type=jnp.float32
    )
    return exchange_matrix


def solution(mesh):
    return jax.shard_map(
        shards,
        mesh=mesh,
        in_specs=(
            P(("groups", "row"), None),
            P(("groups", "row"), None),
            P(("groups", "row"), None),
        ),
        out_specs=P("groups", "row"),
        check_vma=False,
    )
```

profile of v0, /device:TPU:0, one launch (start us, length us, event | category | flops | bytes accessed | tf_op | source)
XLA Modules:
  0.0 133.2 jit_solution(10812226006285130068)
XLA Ops:
  6.5 0.0 all-gather.3.cloned.1.call-start
  6.5 0.7 all-gather.3.cloned.1.call-update
  7.3 0.0 all-gather.5.cloned.1.call-start
  7.3 0.7 all-gather.5.cloned.1.call-update
  8.0 45.7 %all-gather.3.cloned.1.call-done = bf16[2048,512]{1,0:T(8,128)(2,1)} async-done(((bf16[128,512]{1,0:T(8,128)(2,1)}), bf16[2048,512]{1,0:T(8,128)(2,1)}) %all-gather.3.cloned.1.call-update) | async-done | bytes 2097168 | tf_op jit(solution)/shard_map/all_gather | solution.py:10
  53.7 51.3 %all-gather.5.cloned.1.call-done = bf16[2048,1024]{1,0:T(8,128)(2,1)} async-done(((bf16[128,1024]{1,0:T(8,128)(2,1)}), bf16[2048,1024]{1,0:T(8,128)(2,1)}) %all-gather.5.cloned.1.call-update) | async-done | bytes 4194320 | tf_op jit(solution)/shard_map/all_gather | solution.py:15
  105.0 4.4 %convolution_convert_fusion = bf16[128,1024]{1,0:T(8,128)(2,1)S(1)} fusion(bf16[2048,1024]{1,0:T(8,128)(2,1)} %all-gather.5.cloned.1.call-done, bf16[128,512]{1,0:T(8,128)(2,1)} %param.3, bf16[2048,512]{1,0:T(8,128)(2,1)} %all-gather.3.cloned.1.call-done, bf16[128,2048]{1,0:T(8,128)(2,1)} %param.5), kind=kOutput, calls=%fused_computation.2 | convolution fusion | flops 806223872 | bytes 7208960 | tf_op jit(solution)/shard_map/dot_general | solution.py:16
  109.4 0.2 copy.4
  109.6 13.1 %all_to_all.19 = bf16[128,16,64]{0,2,1:T(8,128)(2,1)S(1)} all-to-all(bf16[128,16,64]{0,2,1:T(8,128)(2,1)S(1)} %bitcast.15), channel_id=1, replica_groups=mesh['groups'=2,'row'=16] {'row'}, dimensions={1} | all-to-all | bytes 524288 | tf_op jit(solution)/shard_map/all_to_all | solution.py:19
  122.6 3.7 %convolution_bitcast_fusion = f32[1024,64]{0,1:T(8,128)} fusion(bf16[2048,1024]{1,0:T(8,128)(2,1)} %all-gather.5.cloned.1.call-done, bf16[128,16,64]{0,2,1:T(8,128)(2,1)S(1)} %all_to_all.19), kind=kOutput, calls=%fused_computation.3 | convolution fusion | flops 268435456 | bytes 4718592 | tf_op jit(solution)/shard_map/dot_general | solution.py:20
Async XLA Ops:
  6.5 47.2 %all-gather.3.cloned.1.call-start = ((), (), s32[]{:S(2)}) async-start(), calls=%async_computation.1 | async-start | bytes 2228224 | tf_op jit(solution)/shard_map/all_gather | solution.py:10
  7.3 97.7 %all-gather.5.cloned.1.call-start = ((), (), s32[]{:S(2)}) async-start(), calls=%async_computation.2 | async-start | bytes 4456448 | tf_op jit(solution)/shard_map/all_gather | solution.py:15
Sparse Core Ops, SparseCore 0:
  9.5 44.1 all-gather.2
  55.9 49.0 all-gather.4
where the time goes:
time: 133 us
  waiting for transfers between devices  98.4 us (74%)
  between operations  13.4 us (10%)
  blocking collectives  13.1 us (10%)
  matrix products  8.13 us (6%)
    all_gather x1, waiting for transfers between devices, shards(): whole_basis = lax.all_gather(basis, 'row', axis=0, tiled=True)  51.3 us
    all_gather x1, waiting for transfers between devices, shards(): lax.all_gather(orbitals, 'row', axis=0, tiled=True)  45.7 us
    all_to_all x1, blocking collectives, shards(): lax.all_to_all(applied, 'row', split_axis=1, concat_axis=0, tiled=True)  13.1 us
    dot_general x1, matrix products, shards(): jnp.dot(weighted, whole_basis, preferred_element_type=jnp.float32)  4.39 us
    dot_general x1, matrix products, shards(): lax.dot_general(whole_basis, received, (((0,), (0,)), ((), ())), preferre...  3.73 us
  transfers between devices with their start and end apart: 2, of which 2 were waited for; matrix products, arithmetic and copies ran while one was open for 0% of the time, Pallas kernels for 0%

commit v1 on v0

--- a/solution.py
+++ b/solution.py
@@ -12,7 +12,12 @@
         preferred_element_type=jnp.float32,
     )
     weighted = (density * kernel.astype(jnp.float32)).astype(jnp.bfloat16)
-    whole_basis = lax.all_gather(basis, "row", axis=0, tiled=True)
+    ring = [basis]
+    for hop in range(15):
+        ring.append(lax.ppermute(ring[-1], "row", [(dev, (dev + 1) % 16) for dev in range(16)]))
+    whole_basis = jnp.roll(
+        jnp.concatenate(ring[::-1], axis=0), (lax.axis_index("row") + 1) * ring[0].shape[0], axis=0
+    )
     applied = jnp.dot(weighted, whole_basis, preferred_element_type=jnp.float32).astype(
         jnp.bfloat16
     )

time: 133 us -> 200 us (1.50)
  waiting for transfers between devices: 98.4 us -> 134 us
  local copies, waits for them, and re-layouts: 0.17 us -> 29.7 us
    ppermute x0 -> x15, waiting for transfers between devices: none -> 129 us  [shards(): lax.ppermute(ring[-1], 'row', [(dev, (dev + 1) % 16) for dev in range(16)])]
    all_gather x1 -> x0, waiting for transfers between devices: 51.3 us -> none  [shards(): whole_basis = lax.all_gather(basis, 'row', axis=0, tiled=True)]
    all_gather x1, waiting for transfers between devices: 45.7 us -> 5.54 us  [shards(): lax.all_gather(orbitals, 'row', axis=0, tiled=True)]
    unnamed x0 -> x39, local copies, waits for them, and re-layouts: none -> 28.8 us
  transfers between devices with their start and end apart: 2 -> 16, of which waited for: 2 -> 16; matrix products, arithmetic and copies ran while one was open for 0% -> 14% of each run, Pallas kernels for 0% -> 0%
where the time goes in v1:
time: 200 us; the launch traced here: 199 us
  waiting for transfers between devices  134 us (67%)
  local copies, waits for them, and re-layouts  29.7 us (15%)
  between operations  13.5 us (7%)
  blocking collectives  13.2 us (7%)
  matrix products  8.12 us (4%)
    ppermute x15, waiting for transfers between devices, shards(): lax.ppermute(ring[-1], 'row', [(dev, (dev + 1) % 16) for dev in range(16)])  129 us
    unnamed x39, local copies, waits for them, and re-layouts  28.8 us
    all_to_all x1, blocking collectives, shards(): lax.all_to_all(applied, 'row', split_axis=1, concat_axis=0, tiled=True)  13.2 us
    all_gather x1, waiting for transfers between devices, shards(): lax.all_gather(orbitals, 'row', axis=0, tiled=True)  5.54 us
    dot_general x1, matrix products, shards(): jnp.dot(weighted, whole_basis, preferred_element_type=jnp.float32)  4.38 us
  transfers between devices with their start and end apart: 16, of which 16 were waited for; matrix products, arithmetic and copies ran while one was open for 14% of the time, Pallas kernels for 0%

profile of v1, /device:TPU:0, one launch (start us, length us, event | category | flops | bytes accessed | tf_op | source)
XLA Modules:
  0.0 199.2 jit_solution(10108571037911150639)
XLA Ops:
  7.0 9.3 %collective-permute-done = bf16[128,1024]{1,0:T(8,128)(2,1)S(1)} collective-permute-done((bf16[128,1024]{1,0:T(8,128)(2,1)}, bf16[128,1024]{1,0:T(8,128)(2,1)S(1)}, u32[]{:S(2)}, u32[]{:S(2)}) %collective-permute-start) | collective-permute-done | bytes 262176 | tf_op jit(solution)/shard_map/ppermute | solution.py:17
  16.3 8.5 %collective-permute-done.1 = bf16[128,1024]{1,0:T(8,128)(2,1)S(1)} collective-permute-done((bf16[128,1024]{1,0:T(8,128)(2,1)S(1)}, bf16[128,1024]{1,0:T(8,128)(2,1)S(1)}, u32[]{:S(2)}, u32[]{:S(2)}) %collective-permute-start.1) | collective-permute-done | bytes 262176 | tf_op jit(solution)/shard_map/ppermute | solution.py:17
  24.8 8.5 %collective-permute-done.2 = bf16[128,1024]{1,0:T(8,128)(2,1)S(1)} collective-permute-done((bf16[128,1024]{1,0:T(8,128)(2,1)S(1)}, bf16[128,1024]{1,0:T(8,128)(2,1)S(1)}, u32[]{:S(2)}, u32[]{:S(2)}) %collective-permute-start.2) | collective-permute-done | bytes 262176 | tf_op jit(solution)/shard_map/ppermute | solution.py:17
  33.3 8.5 %collective-permute-done.3 = bf16[128,1024]{1,0:T(8,128)(2,1)S(1)} collective-permute-done((bf16[128,1024]{1,0:T(8,128)(2,1)S(1)}, bf16[128,1024]{1,0:T(8,128)(2,1)S(1)}, u32[]{:S(2)}, u32[]{:S(2)}) %collective-permute-start.3) | collective-permute-done | bytes 262176 | tf_op jit(solution)/shard_map/ppermute | solution.py:17
  41.8 8.5 %collective-permute-done.4 = bf16[128,1024]{1,0:T(8,128)(2,1)S(1)} collective-permute-done((bf16[128,1024]{1,0:T(8,128)(2,1)S(1)}, bf16[128,1024]{1,0:T(8,128)(2,1)S(1)}, u32[]{:S(2)}, u32[]{:S(2)}) %collective-permute-start.4) | collective-permute-done | bytes 262176 | tf_op jit(solution)/shard_map/ppermute | solution.py:17
  50.3 8.5 %collective-permute-done.5 = bf16[128,1024]{1,0:T(8,128)(2,1)S(1)} collective-permute-done((bf16[128,1024]{1,0:T(8,128)(2,1)S(1)}, bf16[128,1024]{1,0:T(8,128)(2,1)S(1)}, u32[]{:S(2)}, u32[]{:S(2)}) %collective-permute-start.5) | collective-permute-done | bytes 262176 | tf_op jit(solution)/shard_map/ppermute | solution.py:17
  58.8 8.5 %collective-permute-done.6 = bf16[128,1024]{1,0:T(8,128)(2,1)S(1)} collective-permute-done((bf16[128,1024]{1,0:T(8,128)(2,1)S(1)}, bf16[128,1024]{1,0:T(8,128)(2,1)S(1)}, u32[]{:S(2)}, u32[]{:S(2)}) %collective-permute-start.6) | collective-permute-done | bytes 262176 | tf_op jit(solution)/shard_map/ppermute | solution.py:17
  67.3 8.5 %collective-permute-done.7 = bf16[128,1024]{1,0:T(8,128)(2,1)S(1)} collective-permute-done((bf16[128,1024]{1,0:T(8,128)(2,1)S(1)}, bf16[128,1024]{1,0:T(8,128)(2,1)S(1)}, u32[]{:S(2)}, u32[]{:S(2)}) %collective-permute-start.7) | collective-permute-done | bytes 262176 | tf_op jit(solution)/shard_map/ppermute | solution.py:17
  75.8 8.5 %collective-permute-done.8 = bf16[128,1024]{1,0:T(8,128)(2,1)S(1)} collective-permute-done((bf16[128,1024]{1,0:T(8,128)(2,1)S(1)}, bf16[128,1024]{1,0:T(8,128)(2,1)S(1)}, u32[]{:S(2)}, u32[]{:S(2)}) %collective-permute-start.8) | collective-permute-done | bytes 262176 | tf_op jit(solution)/shard_map/ppermute | solution.py:17
  84.3 8.5 %collective-permute-done.9 = bf16[128,1024]{1,0:T(8,128)(2,1)S(1)} collective-permute-done((bf16[128,1024]{1,0:T(8,128)(2,1)S(1)}, bf16[128,1024]{1,0:T(8,128)(2,1)S(1)}, u32[]{:S(2)}, u32[]{:S(2)}) %collective-permute-start.9) | collective-permute-done | bytes 262176 | tf_op jit(solution)/shard_map/ppermute | solution.py:17
  92.8 8.5 %collective-permute-done.10 = bf16[128,1024]{1,0:T(8,128)(2,1)S(1)} collective-permute-done((bf16[128,1024]{1,0:T(8,128)(2,1)S(1)}, bf16[128,1024]{1,0:T(8,128)(2,1)S(1)}, u32[]{:S(2)}, u32[]{:S(2)}) %collective-permute-start.10) | collective-permute-done | bytes 262176 | tf_op jit(solution)/shard_map/ppermute | solution.py:17
  101.3 8.5 %collective-permute-done.11 = bf16[128,1024]{1,0:T(8,128)(2,1)S(1)} collective-permute-done((bf16[128,1024]{1,0:T(8,128)(2,1)S(1)}, bf16[128,1024]{1,0:T(8,128)(2,1)S(1)}, u32[]{:S(2)}, u32[]{:S(2)}) %collective-permute-start.11) | collective-permute-done | bytes 262176 | tf_op jit(solution)/shard_map/ppermute | solution.py:17
  109.8 8.5 %collective-permute-done.12 = bf16[128,1024]{1,0:T(8,128)(2,1)S(1)} collective-permute-done((bf16[128,1024]{1,0:T(8,128)(2,1)S(1)}, bf16[128,1024]{1,0:T(8,128)(2,1)S(1)}, u32[]{:S(2)}, u32[]{:S(2)}) %collective-permute-start.12) | collective-permute-done | bytes 262176 | tf_op jit(solution)/shard_map/ppermute | solution.py:17
  119.0 8.6 %collective-permute-done.13 = bf16[128,1024]{1,0:T(8,128)(2,1)} collective-permute-done((bf16[128,1024]{1,0:T(8,128)(2,1)S(1)}, bf16[128,1024]{1,0:T(8,128)(2,1)}, u32[]{:S(2)}, u32[]{:S(2)}) %collective-permute-start.13) | collective-permute-done | bytes 262176 | tf_op jit(solution)/shard_map/ppermute | solution.py:17
  127.7 8.7 %collective-permute-done.14 = bf16[128,1024]{1,0:T(8,128)(2,1)} collective-permute-done((bf16[128,1024]{1,0:T(8,128)(2,1)}, bf16[128,1024]{1,0:T(8,128)(2,1)}, u32[]{:S(2)}, u32[]{:S(2)}) %collective-permute-start.14) | collective-permute-done | bytes 262176 | tf_op jit(solution)/shard_map/ppermute | solution.py:17
  136.4 1.7 constant_dynamic-update-slice_fusion.31
  138.1 1.7 constant_dynamic-update-slice_fusion.30
  139.7 1.7 constant_dynamic-update-slice_fusion.29
  144.2 0.7 constant_dynamic-update-slice_fusion.24
  146.4 0.7 constant_dynamic-update-slice_fusion.21
  150.0 1.7 constant_dynamic-update-slice_fusion.16
  151.6 1.7 constant_dynamic-update-slice_fusion.15
  153.3 1.8 constant_dynamic-update-slice_fusion.14
  155.1 0.7 constant_dynamic-update-slice_fusion.13
  159.4 0.7 constant_dynamic-update-slice_fusion.7
  160.8 0.7 constant_dynamic-update-slice_fusion.5
  163.7 0.8 constant_dynamic-update-slice_fusion.1
  164.5 0.7 constant_dynamic-update-slice_fusion
  165.2 5.5 %all-gather.2.cloned.1.call-done = bf16[2048,512]{1,0:T(8,128)(2,1)} async-done(((bf16[128,512]{1,0:T(8,128)(2,1)}), bf16[2048,512]{1,0:T(8,128)(2,1)}) %all-gather.2.cloned.1.call-update) | async-done | bytes 2097168 | tf_op jit(solution)/shard_map/all_gather | solution.py:10
  170.8 4.4 %fusion.5 = bf16[128,1024]{1,0:T(8,128)(2,1)S(1)} fusion(bf16[4096,1024]{1,0:T(8,128)(2,1)} %constant_dynamic-update-slice_fusion, s32[]{:T(128)S(6)} %select_n.14, bf16[128,512]{1,0:T(8,128)(2,1)S(1)} %copy-done.3, bf16[2048,512]{1,0:T(8,128)(2,1)} %all-gather.2.cloned.1.call-done, bf16[128,2048]{1,0:T(8,128)(2,1)} %param.5), kind=kOutput, calls=%fused_computation.6 | convolution fusion | flops 806223872 | bytes 7208964 | tf_op jit(solution)/shard_map/dot_general | solution.py:21
  175.3 13.2 %all_to_all.19 = bf16[128,16,64]{0,2,1:T(8,128)(2,1)S(1)} all-to-all(bf16[128,16,64]{0,2,1:T(8,128)(2,1)S(1)} %bitcast.11), channel_id=1, replica_groups=mesh['groups'=2,'row'=16] {'row'}, dimensions={1} | all-to-all | bytes 524288 | tf_op jit(solution)/shard_map/all_to_all | solution.py:24
  188.6 3.7 %fusion = f32[1024,64]{0,1:T(8,128)} fusion(bf16[4096,1024]{1,0:T(8,128)(2,1)} %constant_dynamic-update-slice_fusion, s32[]{:T(128)S(6)} %select_n.14, bf16[128,16,64]{0,2,1:T(8,128)(2,1)S(1)} %all_to_all.19), kind=kOutput, calls=%fused_computation | convolution fusion | flops 268435456 | bytes 4718596 | tf_op jit(solution)/shard_map/dot_general | solution.py:25
  (45 shorter events, 15.0 us)
Async XLA Ops:
  6.5 157.9 %copy-start = (bf16[128,1024]{1,0:T(8,128)(2,1)S(1)}, bf16[128,1024]{1,0:T(8,128)(2,1)}, u32[]{:S(2)}) copy-start(bf16[128,1024]{1,0:T(8,128)(2,1)} %param.4) | copy-start | bytes 786436
  6.5 164.2 %all-gather.2.cloned.1.call-start = ((), (), s32[]{:S(2)}) async-start(), calls=%async_computation.1 | async-start | bytes 2228224 | tf_op jit(solution)/shard_map/all_gather | solution.py:10
  6.5 9.8 %collective-permute-start = (bf16[128,1024]{1,0:T(8,128)(2,1)}, bf16[128,1024]{1,0:T(8,128)(2,1)S(1)}, u32[]{:S(2)}, u32[]{:S(2)}) collective-permute-start(bf16[128,1024]{1,0:T(8,128)(2,1)} %param.4), channel_id=1, source_target_pairs={{0,1},{1,2},{2,3},{3,4},{4,5},{5,6},{6,7},{7,8},{8,9},{9,10},{10,1... | collective-permute-start | bytes 786440 | tf_op jit(solution)/shard_map/ppermute | solution.py:17
  16.3 8.5 %collective-permute-start.1 = (bf16[128,1024]{1,0:T(8,128)(2,1)S(1)}, bf16[128,1024]{1,0:T(8,128)(2,1)S(1)}, u32[]{:S(2)}, u32[]{:S(2)}) collective-permute-start(bf16[128,1024]{1,0:T(8,128)(2,1)S(1)} %collective-permute-done), channel_id=1, source_target_pairs={{0,1},{1,2},{2,3},{3,4},{4,5},{5,6},{6,7},{7,8},{8,9},{9,10},{10,1... | collective-permute-start | bytes 786440 | tf_op jit(solution)/shard_map/ppermute | solution.py:17
  24.8 8.5 %collective-permute-start.2 = (bf16[128,1024]{1,0:T(8,128)(2,1)S(1)}, bf16[128,1024]{1,0:T(8,128)(2,1)S(1)}, u32[]{:S(2)}, u32[]{:S(2)}) collective-permute-start(bf16[128,1024]{1,0:T(8,128)(2,1)S(1)} %collective-permute-done.1), channel_id=1, source_target_pairs={{0,1},{1,2},{2,3},{3,4},{4,5},{5,6},{6,7},{7,8},{8,9},{9,10},{10,1... | collective-permute-start | bytes 786440 | tf_op jit(solution)/shard_map/ppermute | solution.py:17
  33.3 8.5 %collective-permute-start.3 = (bf16[128,1024]{1,0:T(8,128)(2,1)S(1)}, bf16[128,1024]{1,0:T(8,128)(2,1)S(1)}, u32[]{:S(2)}, u32[]{:S(2)}) collective-permute-start(bf16[128,1024]{1,0:T(8,128)(2,1)S(1)} %collective-permute-done.2), channel_id=1, source_target_pairs={{0,1},{1,2},{2,3},{3,4},{4,5},{5,6},{6,7},{7,8},{8,9},{9,10},{10,1... | collective-permute-start | bytes 786440 | tf_op jit(solution)/shard_map/ppermute | solution.py:17
  41.8 8.5 %collective-permute-start.4 = (bf16[128,1024]{1,0:T(8,128)(2,1)S(1)}, bf16[128,1024]{1,0:T(8,128)(2,1)S(1)}, u32[]{:S(2)}, u32[]{:S(2)}) collective-permute-start(bf16[128,1024]{1,0:T(8,128)(2,1)S(1)} %collective-permute-done.3), channel_id=1, source_target_pairs={{0,1},{1,2},{2,3},{3,4},{4,5},{5,6},{6,7},{7,8},{8,9},{9,10},{10,1... | collective-permute-start | bytes 786440 | tf_op jit(solution)/shard_map/ppermute | solution.py:17
  50.3 8.5 %collective-permute-start.5 = (bf16[128,1024]{1,0:T(8,128)(2,1)S(1)}, bf16[128,1024]{1,0:T(8,128)(2,1)S(1)}, u32[]{:S(2)}, u32[]{:S(2)}) collective-permute-start(bf16[128,1024]{1,0:T(8,128)(2,1)S(1)} %collective-permute-done.4), channel_id=1, source_target_pairs={{0,1},{1,2},{2,3},{3,4},{4,5},{5,6},{6,7},{7,8},{8,9},{9,10},{10,1... | collective-permute-start | bytes 786440 | tf_op jit(solution)/shard_map/ppermute | solution.py:17
  58.8 8.5 %collective-permute-start.6 = (bf16[128,1024]{1,0:T(8,128)(2,1)S(1)}, bf16[128,1024]{1,0:T(8,128)(2,1)S(1)}, u32[]{:S(2)}, u32[]{:S(2)}) collective-permute-start(bf16[128,1024]{1,0:T(8,128)(2,1)S(1)} %collective-permute-done.5), channel_id=1, source_target_pairs={{0,1},{1,2},{2,3},{3,4},{4,5},{5,6},{6,7},{7,8},{8,9},{9,10},{10,1... | collective-permute-start | bytes 786440 | tf_op jit(solution)/shard_map/ppermute | solution.py:17
  67.3 8.5 %collective-permute-start.7 = (bf16[128,1024]{1,0:T(8,128)(2,1)S(1)}, bf16[128,1024]{1,0:T(8,128)(2,1)S(1)}, u32[]{:S(2)}, u32[]{:S(2)}) collective-permute-start(bf16[128,1024]{1,0:T(8,128)(2,1)S(1)} %collective-permute-done.6), channel_id=1, source_target_pairs={{0,1},{1,2},{2,3},{3,4},{4,5},{5,6},{6,7},{7,8},{8,9},{9,10},{10,1... | collective-permute-start | bytes 786440 | tf_op jit(solution)/shard_map/ppermute | solution.py:17
  75.8 8.5 %collective-permute-start.8 = (bf16[128,1024]{1,0:T(8,128)(2,1)S(1)}, bf16[128,1024]{1,0:T(8,128)(2,1)S(1)}, u32[]{:S(2)}, u32[]{:S(2)}) collective-permute-start(bf16[128,1024]{1,0:T(8,128)(2,1)S(1)} %collective-permute-done.7), channel_id=1, source_target_pairs={{0,1},{1,2},{2,3},{3,4},{4,5},{5,6},{6,7},{7,8},{8,9},{9,10},{10,1... | collective-permute-start | bytes 786440 | tf_op jit(solution)/shard_map/ppermute | solution.py:17
  84.3 8.5 %collective-permute-start.9 = (bf16[128,1024]{1,0:T(8,128)(2,1)S(1)}, bf16[128,1024]{1,0:T(8,128)(2,1)S(1)}, u32[]{:S(2)}, u32[]{:S(2)}) collective-permute-start(bf16[128,1024]{1,0:T(8,128)(2,1)S(1)} %collective-permute-done.8), channel_id=1, source_target_pairs={{0,1},{1,2},{2,3},{3,4},{4,5},{5,6},{6,7},{7,8},{8,9},{9,10},{10,1... | collective-permute-start | bytes 786440 | tf_op jit(solution)/shard_map/ppermute | solution.py:17
  92.8 8.5 %collective-permute-start.10 = (bf16[128,1024]{1,0:T(8,128)(2,1)S(1)}, bf16[128,1024]{1,0:T(8,128)(2,1)S(1)}, u32[]{:S(2)}, u32[]{:S(2)}) collective-permute-start(bf16[128,1024]{1,0:T(8,128)(2,1)S(1)} %collective-permute-done.9), channel_id=1, source_target_pairs={{0,1},{1,2},{2,3},{3,4},{4,5},{5,6},{6,7},{7,8},{8,9},{9,10},{10,1... | collective-permute-start | bytes 786440 | tf_op jit(solution)/shard_map/ppermute | solution.py:17
  101.3 8.5 %collective-permute-start.11 = (bf16[128,1024]{1,0:T(8,128)(2,1)S(1)}, bf16[128,1024]{1,0:T(8,128)(2,1)S(1)}, u32[]{:S(2)}, u32[]{:S(2)}) collective-permute-start(bf16[128,1024]{1,0:T(8,128)(2,1)S(1)} %collective-permute-done.10), channel_id=1, source_target_pairs={{0,1},{1,2},{2,3},{3,4},{4,5},{5,6},{6,7},{7,8},{8,9},{9,10},{10,1... | collective-permute-start | bytes 786440 | tf_op jit(solution)/shard_map/ppermute | solution.py:17
  109.8 8.5 %collective-permute-start.12 = (bf16[128,1024]{1,0:T(8,128)(2,1)S(1)}, bf16[128,1024]{1,0:T(8,128)(2,1)S(1)}, u32[]{:S(2)}, u32[]{:S(2)}) collective-permute-start(bf16[128,1024]{1,0:T(8,128)(2,1)S(1)} %collective-permute-done.11), channel_id=1, source_target_pairs={{0,1},{1,2},{2,3},{3,4},{4,5},{5,6},{6,7},{7,8},{8,9},{9,10},{10,1... | collective-permute-start | bytes 786440 | tf_op jit(solution)/shard_map/ppermute | solution.py:17
  118.3 0.7 copy-start.1
  119.0 8.6 %collective-permute-start.13 = (bf16[128,1024]{1,0:T(8,128)(2,1)S(1)}, bf16[128,1024]{1,0:T(8,128)(2,1)}, u32[]{:S(2)}, u32[]{:S(2)}) collective-permute-start(bf16[128,1024]{1,0:T(8,128)(2,1)S(1)} %collective-permute-done.12), channel_id=1, source_target_pairs={{0,1},{1,2},{2,3},{3,4},{4,5},{5,6},{6,7},{7,8},{8,9},{9,10},{10,1... | collective-permute-start | bytes 786440 | tf_op jit(solution)/shard_map/ppermute | solution.py:17
  127.6 8.8 %collective-permute-start.14 = (bf16[128,1024]{1,0:T(8,128)(2,1)}, bf16[128,1024]{1,0:T(8,128)(2,1)}, u32[]{:S(2)}, u32[]{:S(2)}) collective-permute-start(bf16[128,1024]{1,0:T(8,128)(2,1)} %collective-permute-done.13), channel_id=1, source_target_pairs={{0,1},{1,2},{2,3},{3,4},{4,5},{5,6},{6,7},{7,8},{8,9},{9,10},{10,1... | collective-permute-start | bytes 786440 | tf_op jit(solution)/shard_map/ppermute | solution.py:17
  127.6 27.5 %copy-start.2 = (bf16[128,1024]{1,0:T(8,128)(2,1)S(1)}, bf16[128,1024]{1,0:T(8,128)(2,1)}, u32[]{:S(2)}) copy-start(bf16[128,1024]{1,0:T(8,128)(2,1)} %copy-done.1) | copy-start | bytes 786436
  127.6 43.1 %copy-start.3 = (bf16[128,512]{1,0:T(8,128)(2,1)S(1)}, bf16[128,512]{1,0:T(8,128)(2,1)}, u32[]{:S(2)}) copy-start(bf16[128,512]{1,0:T(8,128)(2,1)} %param.3) | copy-start | bytes 393220
Sparse Core Ops, SparseCore 0:
  127.7 42.9 all-gather.1
